TPU v7x, 512 devices: a whole 4x4x16 slice. The times are simulated.
512 devices in a mesh: req: 64 (over x, z), head: 8 (over y, core).
Axes of the slice: x: 4, y: 4, z: 16, core: 2. Of those that a mesh axis runs over, the one named last changes fastest.
Arguments:
- tokens: bfloat16 [320, 1024], P('req'), may hold values from -6 to 6
- norm_gain: float32 [1024], replicated, may hold values from 0.1 to 1.9
- w_qkv: bfloat16 [1024, 8, 384], P(None, 'head'), may hold values from -0.1875 to 0.1875
- persist_kv: bfloat16 [8, 16, 256], P('head'), may hold values from -9 to 9
- memory: bfloat16 [64, 8, 128, 128], P('req', 'head'), may hold values from -0.5 to 0.5
- cache_kv: bfloat16 [512, 512, 8, 256], P('req', None, 'head')
- piece_owner: int32 [512], P('req'), may hold values from 0 to 63, as said below
- piece_len: int32 [512], P('req'), may hold values from 1 to 512, as said below
- w_out: bfloat16 [8, 128, 1024], P('head'), may hold values from -0.1875 to 0.1875
Outputs:
- layer_out: bfloat16 [320, 1024], P('req', 'head')
Inputs may be any that keep to these rules, and one draw needn't show every extreme that they name: `piece_owner`: every request owns 1 to 16 pieces, and one request owns exactly 16. `piece_len`: some piece is full.
All inputs are finite; a program needn't handle non-finite values.
Results may differ from a plain program's by a relative error of at most 0.009.
The roundings to bfloat16 on the way count: a program that leaves them out, or rounds other values in their place, can miss the bound.
Values may be sent and summed in bfloat16 or wider, within the bound.
No kernel may reach another device: no remote copies, remote signals or barrier semaphores. Data moves between devices by JAX's collectives and lax.ppermute only.
A program may use at most 64 MiB of HBM per device.

v0:
```python
import jax
import jax.numpy as jnp
from jax import lax
from jax.sharding import PartitionSpec as P

DH = 128
NP = 16
Q = 5
PIECE = 512
masked_score = -1e30
norm_eps = 1e-06


def merged(shard, axis, combine):
    everything = jax.tree.map(lambda part: lax.all_gather(part, axis), shard)
    leading = jax.tree.map(lambda part: part[0], everything)

    def step(k, so_far):
        return combine(so_far, jax.tree.map(lambda part: part[k], everything))

    return lax.fori_loop(1, lax.axis_size(axis), step, leading)


def join_parts(first, second):
    peak = jnp.maximum(first[0], second[0])
    scale_one = jnp.exp(first[0] - peak)
    scale_two = jnp.exp(second[0] - peak)
    total = first[1] * scale_one + second[1] * scale_two
    summed = first[2] * scale_one[..., None] + second[2] * scale_two[..., None]
    return (peak, total, summed)


def dense_parts(peaks, totals, summed, piece_owner, total_reqs):
    f32 = jnp.float32
    onehot = piece_owner[:, None] == jnp.arange(total_reqs, dtype=jnp.int32)[None, :]
    peak_dev = jnp.max(jnp.where(onehot[:, :, None, None], peaks[:, None], masked_score), axis=0)
    factor = jnp.exp(peaks - peak_dev[piece_owner])
    onehot_f = onehot.astype(f32)
    total_dev = jnp.einsum(
        "sr,shq->rhq", onehot_f, totals * factor, precision=lax.Precision.HIGHEST
    )
    summed_dev = jnp.einsum(
        "sr,shqe->rhqe", onehot_f, summed * factor[..., None], precision=lax.Precision.HIGHEST
    )
    return (peak_dev, total_dev, summed_dev)


def shards(tokens, norm_gain, w_qkv, persist_kv, memory, cache_kv, piece_owner, piece_len, w_out):
    f32 = jnp.float32
    rows = tokens.shape[0]
    heads = w_qkv.shape[1]
    req_dev = memory.shape[0]
    xf = tokens.astype(f32)
    normed = (
        xf * lax.rsqrt(jnp.mean(xf * xf, axis=-1, keepdims=True) + norm_eps) * norm_gain
    ).astype(jnp.bfloat16)
    proj = jnp.einsum("td,dhe->the", normed, w_qkv, preferred_element_type=f32)
    query = (proj[..., :DH] * DH ** (-0.5)).astype(jnp.bfloat16)
    new_key = proj[..., DH : 2 * DH].astype(jnp.bfloat16)
    new_value = proj[..., 2 * DH :].astype(jnp.bfloat16)
    all_query = lax.all_gather(query, "req", axis=0, tiled=True)
    query_all4 = all_query.reshape(-1, Q, heads, DH)
    total_reqs = query_all4.shape[0]
    query_rows = query_all4[piece_owner]
    scores = jnp.einsum(
        "sqhe,skhe->shqk", query_rows, cache_kv[..., :DH], preferred_element_type=f32
    )
    valid = (jnp.arange(PIECE)[None, :] < piece_len[:, None])[:, None, None, :]
    scores = jnp.where(valid, scores, masked_score)
    peaks = jnp.max(scores, axis=-1)
    weight = jnp.where(valid, jnp.exp(scores - peaks[..., None]), 0.0)
    totals = jnp.sum(weight, axis=-1)
    summed = jnp.einsum(
        "shqk,skhe->shqe",
        weight.astype(jnp.bfloat16),
        cache_kv[..., DH:],
        preferred_element_type=f32,
    )
    peak_dev, total_dev, summed_dev = dense_parts(peaks, totals, summed, piece_owner, total_reqs)
    peak_all, total_all, summed_all = merged((peak_dev, total_dev, summed_dev), "req", join_parts)
    start = lax.axis_index("req") * req_dev
    peak_cache = lax.dynamic_slice_in_dim(peak_all, start, req_dev, 0)
    total_cache = lax.dynamic_slice_in_dim(total_all, start, req_dev, 0)
    summed_cache = lax.dynamic_slice_in_dim(summed_all, start, req_dev, 0)
    query4 = query.reshape(req_dev, Q, heads, DH)
    key4 = new_key.reshape(req_dev, Q, heads, DH)
    value4 = new_value.reshape(req_dev, Q, heads, DH)
    score_persist = jnp.einsum(
        "rqhe,hne->rhqn", query4, persist_kv[..., :DH], preferred_element_type=f32
    )
    score_new = jnp.einsum("rqhe,rkhe->rhqk", query4, key4, preferred_element_type=f32)
    causal = jnp.arange(Q)[:, None] >= jnp.arange(Q)[None, :]
    score_new = jnp.where(causal, score_new, masked_score)
    score_own = jnp.concatenate([score_persist, score_new], axis=-1)
    peak_own = jnp.max(score_own, axis=-1)
    weight_own = jnp.exp(score_own - peak_own[..., None])
    total_own = jnp.sum(weight_own, axis=-1)
    rounded_own = weight_own.astype(jnp.bfloat16)
    summed_own = jnp.einsum(
        "rhqn,hne->rhqe", rounded_own[..., :NP], persist_kv[..., DH:], preferred_element_type=f32
    )
    summed_own = summed_own + jnp.einsum(
        "rhqk,rkhe->rhqe", rounded_own[..., NP:], value4, preferred_element_type=f32
    )
    peak_total = jnp.maximum(peak_cache, peak_own)
    scale_cache = jnp.exp(peak_cache - peak_total)
    scale_own = jnp.exp(peak_own - peak_total)
    total_final = total_cache * scale_cache + total_own * scale_own
    summed_final = summed_cache * scale_cache[..., None] + summed_own * scale_own[..., None]
    attended = summed_final / total_final[..., None]
    recalled = jnp.einsum("rqhe,rhef->rhqf", query4, memory, preferred_element_type=f32)
    head_out = (attended + recalled).astype(jnp.bfloat16)
    head_out = jnp.transpose(head_out, (0, 2, 1, 3)).reshape(rows, heads, DH)
    partial_out = jnp.einsum("thd,hdf->tf", head_out, w_out, preferred_element_type=f32)
    return lax.psum_scatter(partial_out, "head", scatter_dimension=1, tiled=True).astype(
        jnp.bfloat16
    )


def solution(mesh):
    in_specs = (
        P("req", None),
        P(),
        P(None, "head", None),
        P("head", None, None),
        P("req", "head", None, None),
        P("req", None, "head", None),
        P("req"),
        P("req"),
        P("head", None, None),
    )
    out_specs = P("req", "head")
    return jax.shard_map(shards, mesh=mesh, in_specs=in_specs, out_specs=out_specs, check_vma=False)
```

profile of v0, /device:TPU:2, one launch (start us, length us, event | category | flops | bytes accessed | tf_op | source)
XLA Modules:
  0.0 403.9 jit_solution(6034953627705232493)
XLA Ops:
  9.0 0.9 fusion.60
  10.0 88.1 %all_gather.21 = bf16[320,1,128]{2,1,0:T(2,128)(2,1)S(1)} all-gather(bf16[5,1,128]{2,1,0:T(2,128)(2,1)S(1)} %copy.57), channel_id=1, replica_groups=mesh['req'=64,'head'=8] {'req'}, dimensions={0}, use_global_device_ids=true | all-gather | bytes 83200 | tf_op jit(solution)/shard_map/all_gather | solution.py:61
  100.0 1.7 fusion.61
  102.8 1.0 fusion.25
  103.9 79.7 %all-gather.3 = f32[64,64,5]{1,2,0:T(8,128)S(1)} all-gather(f32[1,64,5]{1,2,0:T(8,128)S(1)} %bitcast.171), channel_id=2, replica_groups=mesh['req'=64,'head'=8] {'req'}, dimensions={0}, use_global_device_ids=true | all-gather | bytes 83200 | tf_op jit(solution)/shard_map/all_gather | solution.py:15
  184.0 81.1 %all-gather.4 = f32[64,64,5]{1,2,0:T(8,128)S(1)} all-gather(f32[1,64,5]{1,2,0:T(8,128)S(1)} %convolution_bitcast_fusion.1), channel_id=3, replica_groups=mesh['req'=64,'head'=8] {'req'}, dimensions={0}, use_global_device_ids=true | all-gather | bytes 83200 | tf_op jit(solution)/shard_map/all_gather | solution.py:15
  266.9 93.1 %while.19 = (s32[]{:T(128)}, f32[64,1,5]{0,1,2:T(1,128)S(1)}, f32[64,1,5]{0,1,2:T(1,128)S(1)}, f32[64,1,5,128]{3,2,1,0:T(8,128)S(1)}, f32[64,64,1,5]{1,2,3,0:T(1...) while((s32[]{:T(128)}, f32[64,1,5]{0,1,2:T(1,128)S(1)}, ...), condition=%wide.region_5.6_spmd, body=%wide.region_4.5_spmd.sunk | while | flops 124805 | bytes 837271 | solution.py:21
  267.0 0.9 constant_dynamic-slice_fusion.4
  268.5 0.9 constant_dynamic-slice_fusion.4
  270.0 0.9 constant_dynamic-slice_fusion.4
  271.4 0.9 constant_dynamic-slice_fusion.4
  272.9 0.9 constant_dynamic-slice_fusion.4
  274.4 0.9 constant_dynamic-slice_fusion.4
  275.9 0.9 constant_dynamic-slice_fusion.4
  277.4 0.9 constant_dynamic-slice_fusion.4
  278.8 0.9 constant_dynamic-slice_fusion.4
  280.3 0.9 constant_dynamic-slice_fusion.4
  281.8 0.9 constant_dynamic-slice_fusion.4
  283.3 0.9 constant_dynamic-slice_fusion.4
  284.7 0.9 constant_dynamic-slice_fusion.4
  286.2 0.9 constant_dynamic-slice_fusion.4
  287.7 0.9 constant_dynamic-slice_fusion.4
  289.2 0.9 constant_dynamic-slice_fusion.4
  290.7 0.9 constant_dynamic-slice_fusion.4
  292.1 0.9 constant_dynamic-slice_fusion.4
  293.6 0.9 constant_dynamic-slice_fusion.4
  295.1 0.9 constant_dynamic-slice_fusion.4
  301.0 0.9 constant_dynamic-slice_fusion.4
  329.1 0.9 constant_dynamic-slice_fusion.4
  357.2 0.9 constant_dynamic-slice_fusion.4
  361.7 34.1 %reduce-scatter.2.cloned.1.call-done = f32[5,128]{1,0:T(8,128)} async-done(((f32[5,1024]{1,0:T(8,128)}), f32[5,128]{1,0:T(8,128)}) %reduce-scatter.2.cloned.1.call-update) | async-done | bytes 2576 | tf_op jit(solution)/shard_map/reduce_scatter | solution.py:115
  395.8 1.2 convert_element_type.39
  (346 shorter events, 79.0 us)
Async XLA Ops:
  6.5 2.5 copy-start
  6.5 96.3 %copy-start.5 = (s32[8]{0:T(128)S(1)}, s32[8]{0:T(128)}, u32[]{:S(2)}) copy-start(s32[8]{0:T(128)} %param.17) | copy-start | bytes 100
  6.5 96.0 %copy-start.1 = (bf16[8,512,1,256]{3,1,2,0:T(8,128)(2,1)S(1)}, bf16[8,512,1,256]{3,1,2,0:T(8,128)(2,1)}, u32[]{:S(2)}) copy-start(bf16[8,512,1,256]{3,1,2,0:T(8,128)(2,1)} %param.16) | copy-start | bytes 6291460
  6.5 259.3 %all-gather.7.cloned.1.call-start = ((), (), s32[]{:S(2)}) async-start(), calls=%async_computation.2 | async-start | bytes 10649600 | tf_op jit(solution)/shard_map/all_gather | solution.py:15
  99.9 165.7 %copy-start.4 = (bf16[1,16,256]{2,1,0:T(8,128)(2,1)S(1)}, bf16[1,16,256]{2,1,0:T(8,128)(2,1)}, u32[]{:S(2)}) copy-start(bf16[1,16,256]{2,1,0:T(8,128)(2,1)} %param.14) | copy-start | bytes 24580
  103.9 291.9 %reduce-scatter.2.cloned.1.call-start = ((), (), s32[]{:S(2)}) async-start(), calls=%async_computation.1 | async-start | bytes 36864 | tf_op jit(solution)/shard_map/reduce_scatter | solution.py:115
  266.9 93.9 %copy-start.2 = (bf16[1,128,1024]{2,1,0:T(8,128)(2,1)S(1)}, bf16[1,128,1024]{2,1,0:T(8,128)(2,1)}, u32[]{:S(2)}) copy-start(bf16[1,128,1024]{2,1,0:T(8,128)(2,1)} %param.19) | copy-start | bytes 786436
  266.9 93.9 %copy-start.3 = (bf16[1,1,128,128]{3,2,1,0:T(8,128)(2,1)S(1)}, bf16[1,1,128,128]{3,2,1,0:T(8,128)(2,1)}, u32[]{:S(2)}) copy-start(bf16[1,1,128,128]{3,2,1,0:T(8,128)(2,1)} %param.15) | copy-start | bytes 98308
Sparse Core Ops, SparseCore 0:
  104.0 158.7 all-gather.6
  361.8 33.9 reduce-scatter.1
where the time goes:
time: 406 us; the launch traced here: 404 us
  blocking collectives  249 us (61%)
  local copies, waits for them, and re-layouts  74.2 us (18%)
  waiting for transfers between devices  34.2 us (8%)
  other arithmetic  25.4 us (6%)
  between operations  13.6 us (3%)
  matrix products  5.76 us (1%)
    all_gather x2, blocking collectives, merged(): everything = jax.tree.map(lambda part: lax.all_gather(part, axis), shard)  161 us
    all_gather x1, blocking collectives, shards(): all_query = lax.all_gather(query, 'req', axis=0, tiled=True)  88.1 us
    dynamic_slice x63, local copies, waits for them, and re-layouts, step(): return combine(so_far, jax.tree.map(lambda part: part[k], everything))  59.1 us
    reduce_scatter x1, waiting for transfers between devices, shards(): lax.psum_scatter(partial_out, 'head', scatter_dimension=1, tiled=True)  34.1 us
    add x63, other arithmetic, join_parts(): summed = first[2] * scale_one[..., None] + second[2] * scale_two[..., None]  17.9 us
    mul x126, local copies, waits for them, and re-layouts, join_parts(): summed = first[2] * scale_one[..., None] + second[2] * scale_two[..., None]  12.1 us
  transfers between devices with their start and end apart: 2, of which 1 were waited for; matrix products, arithmetic and copies ran while one was open for 0% of the time, Pallas kernels for 0%

commit v1 on v0

--- a/solution.py
+++ b/solution.py
@@ -58,7 +58,10 @@
     query = (proj[..., :DH] * DH ** (-0.5)).astype(jnp.bfloat16)
     new_key = proj[..., DH : 2 * DH].astype(jnp.bfloat16)
     new_value = proj[..., 2 * DH :].astype(jnp.bfloat16)
-    all_query = lax.all_gather(query, "req", axis=0, tiled=True)
+    devices = lax.axis_size("req")
+    blocks = jnp.stack([query for _ in range(devices)])
+    blocks = lax.all_to_all(blocks, "req", split_axis=0, concat_axis=0)
+    all_query = jnp.concatenate(blocks, axis=0)
     query_all4 = all_query.reshape(-1, Q, heads, DH)
     total_reqs = query_all4.shape[0]
     query_rows = query_all4[piece_owner]

time: 406 us -> 348 us (0.86)
  blocking collectives: 249 us -> 161 us
  starting transfers between devices: 0.04 us -> 18.7 us
  waiting for transfers between devices: 34.2 us -> 44.6 us
    all_gather x1 -> x0, blocking collectives: 88.1 us -> none  [shards(): all_query = lax.all_gather(query, 'req', axis=0, tiled=True)]
    all_to_all x0 -> x1, starting transfers between devices: none -> 18.6 us  [shards(): blocks = lax.all_to_all(blocks, 'req', split_axis=0, concat_axis=0)]
    all_to_all x0 -> x1, waiting for transfers between devices: none -> 13.3 us  [shards(): blocks = lax.all_to_all(blocks, 'req', split_axis=0, concat_axis=0)]
  transfers between devices with their start and end apart: 2 -> 3, of which waited for: 1 -> 2; matrix products, arithmetic and copies ran while one was open for 0% -> 1% of each run, Pallas kernels for 0% -> 0%
where the time goes in v1:
time: 348 us; the launch traced here: 346 us
  blocking collectives  161 us (46%)
  local copies, waits for them, and re-layouts  75.6 us (22%)
  waiting for transfers between devices  44.6 us (13%)
  other arithmetic  24.9 us (7%)
  starting transfers between devices  18.7 us (5%)
  between operations  13.6 us (4%)
  matrix products  5.77 us (2%)
    all_gather x2, blocking collectives, merged(): everything = jax.tree.map(lambda part: lax.all_gather(part, axis), shard)  161 us
    dynamic_slice x63, local copies, waits for them, and re-layouts, step(): return combine(so_far, jax.tree.map(lambda part: part[k], everything))  59.1 us
    reduce_scatter x1, waiting for transfers between devices, shards(): lax.psum_scatter(partial_out, 'head', scatter_dimension=1, tiled=True)  31.3 us
    all_to_all x1, starting transfers between devices, shards(): blocks = lax.all_to_all(blocks, 'req', split_axis=0, concat_axis=0)  18.6 us
    add x63, other arithmetic, join_parts(): summed = first[2] * scale_one[..., None] + second[2] * scale_two[..., None]  17.9 us
    all_to_all x1, waiting for transfers between devices, shards(): blocks = lax.all_to_all(blocks, 'req', split_axis=0, concat_axis=0)  13.3 us
    mul x126, local copies, waits for them, and re-layouts, join_parts(): summed = first[2] * scale_one[..., None] + second[2] * scale_two[..., None]  12.1 us
  transfers between devices with their start and end apart: 3, of which 2 were waited for; matrix products, arithmetic and copies ran while one was open for 1% of the time, Pallas kernels for 0%

profile of v1, /device:TPU:2, one launch (start us, length us, event | category | flops | bytes accessed | tf_op | source)
XLA Modules:
  0.0 346.1 jit_solution(5202365427208322558)
XLA Ops:
  6.5 1.0 fusion.20
  8.3 1.0 fusion.57
  10.0 18.6 %all-to-all-start = ((bf16[64,5,1,128]{3,1,2,0:T(8,128)(2,1)}), bf16[64,5,1,128]{3,1,2,0:T(8,128)(2,1)S(1)}, u32[]{:S(2)}, u32[]{:S(2)}) async-start(bf16[64,5,1,128]{3,1,2,0:T(8,128)(2,1)} %stack.2), calls=%async_computation | async-start | bytes 262144 | tf_op jit(solution)/shard_map/all_to_all | solution.py:63
  30.8 13.3 %all-to-all-done = bf16[64,5,1,128]{3,1,2,0:T(8,128)(2,1)S(1)} async-done(((bf16[64,5,1,128]{3,1,2,0:T(8,128)(2,1)}), bf16[64,5,1,128]{3,1,2,0:T(8,128)(2,1)S(1)}, u32[]{:S(2)}, u32[]{:S(2)}) %all-to-all-start) | async-done | bytes 81952 | tf_op jit(solution)/shard_map/all_to_all | solution.py:63
  44.7 1.7 fusion.58
  47.5 1.0 fusion.25
  49.1 80.0 %all-gather.3 = f32[64,64,5]{1,2,0:T(8,128)S(1)} all-gather(f32[1,64,5]{1,2,0:T(8,128)S(1)} %bitcast.166), channel_id=2, replica_groups=mesh['req'=64,'head'=8] {'req'}, dimensions={0}, use_global_device_ids=true | all-gather | bytes 83200 | tf_op jit(solution)/shard_map/all_gather | solution.py:15
  129.5 81.0 %all-gather.4 = f32[64,64,5]{1,2,0:T(8,128)S(1)} all-gather(f32[1,64,5]{1,2,0:T(8,128)S(1)} %convolution_bitcast_fusion.1), channel_id=3, replica_groups=mesh['req'=64,'head'=8] {'req'}, dimensions={0}, use_global_device_ids=true | all-gather | bytes 83200 | tf_op jit(solution)/shard_map/all_gather | solution.py:15
  212.0 93.1 %while.19 = (s32[]{:T(128)}, f32[64,1,5]{0,1,2:T(1,128)S(1)}, f32[64,1,5]{0,1,2:T(1,128)S(1)}, f32[64,1,5,128]{3,2,1,0:T(8,128)S(1)}, f32[64,64,1,5]{1,2,3,0:T(1...) while((s32[]{:T(128)}, f32[64,1,5]{0,1,2:T(1,128)S(1)}, ...), condition=%wide.region_5.6_spmd, body=%wide.region_4.5_spmd.sunk | while | flops 124805 | bytes 837271 | solution.py:21
  212.0 0.9 constant_dynamic-slice_fusion.4
  213.5 0.9 constant_dynamic-slice_fusion.4
  215.0 0.9 constant_dynamic-slice_fusion.4
  216.5 0.9 constant_dynamic-slice_fusion.4
  217.9 0.9 constant_dynamic-slice_fusion.4
  219.4 0.9 constant_dynamic-slice_fusion.4
  220.9 0.9 constant_dynamic-slice_fusion.4
  222.4 0.9 constant_dynamic-slice_fusion.4
  223.9 0.9 constant_dynamic-slice_fusion.4
  225.3 0.9 constant_dynamic-slice_fusion.4
  226.8 0.9 constant_dynamic-slice_fusion.4
  228.3 0.9 constant_dynamic-slice_fusion.4
  229.8 0.9 constant_dynamic-slice_fusion.4
  231.2 0.9 constant_dynamic-slice_fusion.4
  232.7 0.9 constant_dynamic-slice_fusion.4
  234.2 0.9 constant_dynamic-slice_fusion.4
  235.7 0.9 constant_dynamic-slice_fusion.4
  237.2 0.9 constant_dynamic-slice_fusion.4
  238.6 0.9 constant_dynamic-slice_fusion.4
  253.4 0.9 constant_dynamic-slice_fusion.4
  281.5 0.9 constant_dynamic-slice_fusion.4
  306.7 31.3 %reduce-scatter.2.cloned.1.call-done = f32[5,128]{1,0:T(8,128)} async-done(((f32[5,1024]{1,0:T(8,128)}), f32[5,128]{1,0:T(8,128)}) %reduce-scatter.2.cloned.1.call-update) | async-done | bytes 2576 | tf_op jit(solution)/shard_map/reduce_scatter | solution.py:118
  338.0 1.2 convert_element_type.42
  (345 shorter events, 80.8 us)
Async XLA Ops:
  6.5 1.8 copy-start
  6.5 41.0 %copy-start.5 = (s32[8]{0:T(128)S(1)}, s32[8]{0:T(128)}, u32[]{:S(2)}) copy-start(s32[8]{0:T(128)} %param.17) | copy-start | bytes 100
  6.5 40.7 %copy-start.1 = (bf16[8,512,1,256]{3,1,2,0:T(8,128)(2,1)S(1)}, bf16[8,512,1,256]{3,1,2,0:T(8,128)(2,1)}, u32[]{:S(2)}) copy-start(bf16[8,512,1,256]{3,1,2,0:T(8,128)(2,1)} %param.16) | copy-start | bytes 6291460
  8.3 40.6 %copy-start.4 = (bf16[1,16,256]{2,1,0:T(8,128)(2,1)S(1)}, bf16[1,16,256]{2,1,0:T(8,128)(2,1)}, u32[]{:S(2)}) copy-start(bf16[1,16,256]{2,1,0:T(8,128)(2,1)} %param.14) | copy-start | bytes 24580
  10.0 34.2 %all-to-all-start = ((bf16[64,5,1,128]{3,1,2,0:T(8,128)(2,1)}), bf16[64,5,1,128]{3,1,2,0:T(8,128)(2,1)S(1)}, u32[]{:S(2)}, u32[]{:S(2)}) async-start(bf16[64,5,1,128]{3,1,2,0:T(8,128)(2,1)} %stack.2), calls=%async_computation | async-start | bytes 262144 | tf_op jit(solution)/shard_map/all_to_all | solution.py:63
  28.6 182.3 %all-gather.7.cloned.1.call-start = ((), (), s32[]{:S(2)}) async-start(), calls=%async_computation.3 | async-start | bytes 10649600 | tf_op jit(solution)/shard_map/all_gather | solution.py:15
  48.6 289.4 %reduce-scatter.2.cloned.1.call-start = ((), (), s32[]{:S(2)}) async-start(), calls=%async_computation.2 | async-start | bytes 36864 | tf_op jit(solution)/shard_map/reduce_scatter | solution.py:118
  211.9 93.9 %copy-start.2 = (bf16[1,128,1024]{2,1,0:T(8,128)(2,1)S(1)}, bf16[1,128,1024]{2,1,0:T(8,128)(2,1)}, u32[]{:S(2)}) copy-start(bf16[1,128,1024]{2,1,0:T(8,128)(2,1)} %param.19) | copy-start | bytes 786436
  212.0 93.9 %copy-start.3 = (bf16[1,1,128,128]{3,2,1,0:T(8,128)(2,1)S(1)}, bf16[1,1,128,128]{3,2,1,0:T(8,128)(2,1)}, u32[]{:S(2)}) copy-start(bf16[1,1,128,128]{3,2,1,0:T(8,128)(2,1)} %param.15) | copy-start | bytes 98308
Sparse Core Ops, SparseCore 0:
  48.7 155.2 all-gather.6
  306.8 31.0 reduce-scatter.1
